TPU v7x, 128 devices: a whole 4x4x4 slice. The times are simulated.
128 devices in a mesh: patch: 8 (over x, core), proto: 16 (over z, y).
Axes of the slice: x: 4, y: 4, z: 4, core: 2. Of those that a mesh axis runs over, the one named last changes fastest.
Arguments:
- student_feats: bfloat16 [32768, 256], P(('patch', 'proto')), may hold values from -50 to 50
- teacher_feats: bfloat16 [32768, 256], P(('patch', 'proto')), may hold values from -50 to 50
- proto_weight: bfloat16 [256, 131072], P(None, 'proto'), may hold values from -4 to 4
- mask_index: int32 [4096], P(('patch', 'proto')), may hold values from 0 to 255, as said below
- row_weight: bfloat16 [4096], P(('patch', 'proto')), may hold values from 0.5 to 4
Outputs:
- grad_student: float32 [4096, 256], P(('patch', 'proto'))
- grad_proto: float32 [256, 131072], P('patch', 'proto')
- loss: float32 [], replicated
Inputs may be any that keep to these rules, and one draw needn't show every extreme that they name: `mask_index`: entries k * 32 to (k + 1) * 32 - 1 are distinct patch positions of image k, counted from that image's first patch.
All inputs are finite; a program needn't handle non-finite values.
Results may differ from a plain program's by a relative error of at most 0.0057.
Values may be sent and summed in bfloat16 or wider, within the bound.
No kernel may reach another device: no remote copies, remote signals or barrier semaphores. Data moves between devices by JAX's collectives and lax.ppermute only.
A program may use at most 128 MiB of HBM per device.

v0:
```python
import jax
import jax.numpy as jnp
from jax import lax
from jax.sharding import PartitionSpec as P

SK_ITERS = 3
eps = 1e-06
teacher_temp = 0.07
student_temp = 0.1


def unit_rows(values):
    values = values.astype(jnp.float32)
    inverse = lax.rsqrt(jnp.sum(values * values, axis=1) + eps)
    return (values * inverse[:, None], inverse)


def finish(teacher_exp, scale_rows, scale_cols, logits, exp_logits, exp_total, weights):
    codes = teacher_exp * scale_rows[:, None] * scale_cols[None, :]
    student_probs = exp_logits / exp_total[:, None]
    grad_logits = (weights[:, None] * (student_probs - codes)).astype(jnp.bfloat16)
    log_total = jnp.log(exp_total)
    loss_partial = jnp.sum(weights[:, None] * codes * (log_total[:, None] - logits))
    return (grad_logits, loss_partial)


def feature_term(grad_logits, proto_cols):
    return (
        lax.dot_general(
            grad_logits, proto_cols, (((1,), (1,)), ((), ())), preferred_element_type=jnp.float32
        )
        / student_temp
    )


def head_term(student_rows, grad_logits):
    return (
        lax.dot_general(
            student_rows, grad_logits, (((0,), (0,)), ((), ())), preferred_element_type=jnp.float32
        )
        / student_temp
    )


def on_device(student_feats, teacher_feats, proto_weight, mask_index, row_weight):
    highest = lax.Precision.HIGHEST
    unit_student, inverse_student = unit_rows(jnp.take(student_feats, mask_index, axis=0))
    unit_teacher, _ = unit_rows(jnp.take(teacher_feats, mask_index, axis=0))
    own_student = unit_student.astype(jnp.bfloat16)
    own_teacher = unit_teacher.astype(jnp.bfloat16)
    w_float = proto_weight.astype(jnp.float32)
    col_inverse = lax.rsqrt(jnp.sum(w_float * w_float, axis=0) + eps)
    unit_proto = w_float * col_inverse[None, :]
    proto_unit = unit_proto.astype(jnp.bfloat16)
    teacher_rows, student_rows, weights = (
        lax.all_gather(own_teacher, "proto", axis=0, tiled=True),
        lax.all_gather(own_student, "proto", axis=0, tiled=True),
        lax.all_gather(row_weight, "proto", axis=0, tiled=True),
    )
    weights = weights.astype(jnp.float32)
    teacher_exp = jnp.exp(
        jnp.dot(teacher_rows, proto_unit, preferred_element_type=jnp.float32) / teacher_temp
    )
    scale_rows = jnp.ones((teacher_rows.shape[0],), jnp.float32)
    for sweep in range(SK_ITERS):
        col_part = jnp.dot(scale_rows, teacher_exp, precision=highest)
        scale_cols = 1.0 / lax.psum(col_part, "patch")
        row_part = jnp.dot(teacher_exp, scale_cols, precision=highest)
        scale_rows = 1.0 / lax.psum(row_part, "proto")
    logits = jnp.dot(student_rows, proto_unit, preferred_element_type=jnp.float32) / student_temp
    exp_logits = jnp.exp(logits)
    exp_total = lax.psum(jnp.sum(exp_logits, axis=1), "proto")
    grad_logits, loss_partial = finish(
        teacher_exp, scale_rows, scale_cols, logits, exp_logits, exp_total, weights
    )
    feature_grad = lax.psum_scatter(
        feature_term(grad_logits, proto_unit), "proto", scatter_dimension=0, tiled=True
    )
    row_share = proto_unit.shape[0] // lax.axis_size("patch")
    row_offset = lax.axis_index("patch") * row_share
    head_full = lax.psum(head_term(student_rows, grad_logits), "patch")
    inner = jnp.sum(unit_proto * head_full, axis=0)
    whole_grad = col_inverse[None, :] * (head_full - unit_proto * inner[None, :])
    grad_proto = lax.dynamic_slice_in_dim(whole_grad, row_offset, row_share, 0)
    loss_total, weight_total = lax.psum(
        (loss_partial, jnp.sum(row_weight.astype(jnp.float32))), ("patch", "proto")
    )
    grad_student = inverse_student[:, None] * (
        feature_grad - unit_student * jnp.sum(unit_student * feature_grad, axis=1)[:, None]
    )
    return (grad_student, grad_proto, loss_total / weight_total)


def solution(mesh):
    in_specs = (
        P(("patch", "proto"), None),
        P(("patch", "proto"), None),
        P(None, "proto"),
        P(("patch", "proto")),
        P(("patch", "proto")),
    )
    out_specs = (P(("patch", "proto"), None), P("patch", "proto"), P())
    return jax.shard_map(
        on_device, mesh=mesh, in_specs=in_specs, out_specs=out_specs, check_vma=False
    )
```

profile of v0, /device:TPU:1, one launch (start us, length us, event | category | flops | bytes accessed | tf_op | source)
XLA Modules:
  0.0 526.8 jit_solution(3142531026962949100)
XLA Ops:
  8.0 0.0 copy-start
  8.0 0.0 reduce-scatter.2.cloned.1.call-start
  8.1 0.7 compare_select_fusion
  8.7 0.7 compare_and_fusion
  9.4 0.6 gather_fusion
  10.1 1.5 gather_fusion.1
  11.6 0.2 fusion.17
  11.8 0.1 fusion.13
  11.9 20.8 %all_gather.11 = bf16[512,256]{1,0:T(8,128)(2,1)S(1)} all-gather(bf16[32,256]{1,0:T(8,128)(2,1)S(1)} %get-tuple-element.15), channel_id=1, replica_groups=mesh['patch'=8,'proto'=16] {'proto'}, dimensions={0}, use_global_device_ids=true | all-gather | bytes 278528 | tf_op jit(solution)/shard_map/all_gather | solution.py:56
  32.7 3.1 fusion
  35.8 4.5 multiply_exponential_fusion
  40.3 7.9 %fusion.20 = f32[1,8192]{1,0:T(1,128)S(1)} fusion(f32[512,8192]{1,0:T(8,128)S(1)} %multiply_exponential_fusion), kind=kOutput, calls=%fused_computation.41 | convolution fusion | flops 50331648 | bytes 16809984 | tf_op jit(solution)/shard_map/dot_general | solution.py:66
  48.2 26.1 %psum.71 = f32[8192]{0:T(1024)S(1)} all-reduce(f32[8192]{0:T(1024)S(1)} %bitcast.33), channel_id=1, replica_groups=mesh['patch'=8,'proto'=16] {'patch'}, use_global_device_ids=true, to_apply=%region_5.7 | all-reduce | flops 8192 | bytes 65536 | tf_op jit(solution)/shard_map/psum | solution.py:67
  74.4 17.6 %fusion.23 = f32[1,512]{1,0:T(1,128)S(1)} fusion(f32[512,8192]{1,0:T(8,128)} %copy-done.2, f32[8192,1]{0,1:T(1,128)S(1)} %bitcast.29), kind=kOutput, calls=%fused_computation.50 | convolution fusion | flops 50331648 | bytes 16812032 | tf_op jit(solution)/shard_map/dot_general | solution.py:68
  92.0 31.0 %psum.72 = f32[512]{0:T(512)S(1)} all-reduce(f32[512]{0:T(512)S(1)} %bitcast.35), channel_id=1, replica_groups=mesh['patch'=8,'proto'=16] {'proto'}, use_global_device_ids=true, to_apply=%region_6.8 | all-reduce | flops 512 | bytes 4096 | tf_op jit(solution)/shard_map/psum | solution.py:69
  123.0 11.5 %fusion.24 = f32[1,8192]{1,0:T(1,128)S(1)} fusion(f32[512,1]{0,1:T(1,128)S(1)} %bitcast.37, f32[512,8192]{1,0:T(8,128)} %copy-done.2), kind=kOutput, calls=%fused_computation.51 | convolution fusion | flops 50331648 | bytes 16812032 | tf_op jit(solution)/shard_map/dot_general | solution.py:66
  134.5 30.9 %psum.73 = f32[8192]{0:T(1024)S(1)} all-reduce(f32[8192]{0:T(1024)S(1)} %bitcast.30), channel_id=1, replica_groups=mesh['patch'=8,'proto'=16] {'patch'}, use_global_device_ids=true, to_apply=%region_7.9 | all-reduce | flops 8192 | bytes 65536 | tf_op jit(solution)/shard_map/psum | solution.py:67
  165.4 17.6 %fusion.25 = f32[1,512]{1,0:T(1,128)S(1)} fusion(f32[512,8192]{1,0:T(8,128)} %copy-done.2, f32[8192,1]{0,1:T(1,128)S(1)} %bitcast.31), kind=kOutput, calls=%fused_computation.52 | convolution fusion | flops 50331648 | bytes 16812032 | tf_op jit(solution)/shard_map/dot_general | solution.py:68
  183.0 28.5 %psum.74 = f32[512]{0:T(512)S(1)} all-reduce(f32[512]{0:T(512)S(1)} %bitcast.36), channel_id=1, replica_groups=mesh['patch'=8,'proto'=16] {'proto'}, use_global_device_ids=true, to_apply=%region_8.10 | all-reduce | flops 512 | bytes 4096 | tf_op jit(solution)/shard_map/psum | solution.py:69
  211.5 11.5 %fusion.26 = f32[1,8192]{1,0:T(1,128)S(1)} fusion(f32[512,1]{0,1:T(1,128)S(1)} %bitcast.38, f32[512,8192]{1,0:T(8,128)} %copy-done.2), kind=kOutput, calls=%fused_computation.53 | convolution fusion | flops 50331648 | bytes 16812032 | tf_op jit(solution)/shard_map/dot_general | solution.py:66
  223.0 31.0 %psum.75 = f32[8192]{0:T(1024)S(1)} all-reduce(f32[8192]{0:T(1024)S(1)} %bitcast.32), channel_id=1, replica_groups=mesh['patch'=8,'proto'=16] {'patch'}, use_global_device_ids=true, to_apply=%region_9.11 | all-reduce | flops 8192 | bytes 65536 | tf_op jit(solution)/shard_map/psum | solution.py:67
  253.9 0.0 copy-start.3
  254.0 17.8 %fusion.27 = f32[1,512]{1,0:T(1,128)S(1)} fusion(f32[512,8192]{1,0:T(8,128)} %copy-done.2, f32[8192,1]{0,1:T(1,128)S(1)} %bitcast.28), kind=kOutput, calls=%fused_computation.54 | convolution fusion | flops 50331648 | bytes 16812032 | tf_op jit(solution)/shard_map/dot_general | solution.py:68
  271.7 17.8 %all_gather.10 = bf16[512,256]{1,0:T(8,128)(2,1)S(1)} all-gather(bf16[32,256]{1,0:T(8,128)(2,1)S(1)} %get-tuple-element.14), channel_id=1, replica_groups=mesh['patch'=8,'proto'=16] {'proto'}, dimensions={0}, use_global_device_ids=true | all-gather | bytes 278528 | tf_op jit(solution)/shard_map/all_gather | solution.py:57
  289.5 0.0 copy-done.3
  289.5 0.0 copy-start.6
  289.5 7.5 %exponential_reduce_fusion = (f32[512]{0:T(512)S(1)}, f32[512,8192]{1,0:T(8,128)}) fusion(bf16[512,256]{1,0:T(8,128)(2,1)S(1)} %all_gather.10, f32[8192]{0:T(1024)S(1)} %add_rsqrt_fusion, bf16[256,8192]{1,0:T(8,128)(2,1)S(1)} %copy-done.3), kind=kOutput, calls=%fused_computation.6 | convolution fusion | flops 2162163200 | bytes 21268480 | tf_op jit(solution)/shard_map/dot_general | solution.py:70
  297.0 30.9 %all-reduce.2 = (f32[512]{0:T(512)S(1)}, f32[512]{0:T(512)S(1)}) all-reduce(f32[512]{0:T(512)S(1)} %bitcast.34, f32[512]{0:T(512)S(1)} %get-tuple-element.16), channel_id=1, replica_groups=mesh['patch'=8,'proto'=16] {'proto'}, use_global_device_ids=true, to_apply=%region_10.12 | all-reduce | flops 1024 | bytes 8192 | tf_op jit(solution)/shard_map/psum | solution.py:69
  327.9 0.6 dynamic-slice
  329.2 0.0 copy-done.6
  329.2 0.2 dynamic-update-slice
  329.4 29.0 %all-reduce = bf16[512]{0:T(512)(128)(2,1)S(1)} all-reduce(bf16[512]{0:T(512)(128)(2,1)S(1)} %dynamic-update-slice), channel_id=1, replica_groups=mesh['patch'=8,'proto'=16] {'proto'}, use_global_device_ids=true, to_apply=%add | all-reduce | flops 512 | bytes 2048
  358.4 14.4 %multiply_reduce_fusion = (f32[]{:T(128)}, bf16[512,8192]{1,0:T(8,128)(2,1)S(1)}) fusion(f32[512,8192]{1,0:T(8,128)} %copy-done.2, f32[512,8192]{1,0:T(8,128)} %get-tuple-element.17, f32[512]{0:T(512)S(1)} %log.3, f32[8192]{0:T(1024)S(1)} %broadcast_divide_fusion, f32[512]{0:T(512)S(1)} %broadcast_divide_fusion.5, f32[512]{0:T(512)S(1)} %convert_element_type.28, ...), kind=kLoop, calls=%fused_computation.2 | loop fusion | flops 46137344 | bytes 41984004 | tf_op jit(solution)/shard_map/reduce_sum | solution.py:23
  372.9 3.2 copy-done.5
  376.1 3.2 fusion.7
  379.3 0.0 reduce-scatter.2.cloned.1.call-update
  379.3 0.0 all-reduce.5.cloned.1.call-start
  379.4 9.0 %convolution_multiply_fusion = f32[256,8192]{1,0:T(8,128)} fusion(bf16[512,256]{1,0:T(8,128)(2,1)S(1)} %all_gather.10, bf16[512,8192]{1,0:T(8,128)(2,1)} %copy-done.5), kind=kOutput, calls=%fused_computation.7 | convolution fusion | flops 2149580800 | bytes 17039360 | tf_op jit(solution)/shard_map/dot_general | solution.py:38
  388.3 0.0 all-reduce.5.cloned.1.call-update
  388.4 0.6 convert_reduce_fusion
  389.0 85.0 %all-reduce.1 = (f32[]{:T(128)}, f32[]{:T(128)}) all-reduce(f32[]{:T(128)} %get-tuple-element.10, f32[]{:T(128)} %convert_reduce_fusion), channel_id=1, replica_groups=mesh['patch'=8,'proto'=16] {'patch','proto'}, use_global_device_ids=true, to_apply=%region_16.18 | all-reduce | flops 2 | bytes 16 | tf_op jit(solution)/shard_map/psum | solution.py:85
  475.3 0.0 reduce-scatter.2.cloned.1.call-done
  475.3 0.9 fusion.14
  476.2 0.0 copy-start.1
  476.3 1.5 fusion.16
  477.8 32.0 %all-reduce.5.cloned.1.call-done = f32[256,8192]{1,0:T(8,128)} async-done(((f32[256,8192]{1,0:T(8,128)}), f32[256,8192]{1,0:T(8,128)}) %all-reduce.5.cloned.1.call-update) | async-done | bytes 8388624 | tf_op jit(solution)/shard_map/psum | solution.py:81
  509.8 6.0 %multiply_reduce_fusion.1 = (f32[8192]{0:T(1024)S(1)}, f32[256,8192]{1,0:T(8,128)S(1)}) fusion(f32[256,8192]{1,0:T(8,128)} %all-reduce.5.cloned.1.call-done, f32[8192]{0:T(1024)S(1)} %add_rsqrt_fusion, bf16[256,8192]{1,0:T(8,128)(2,1)} %param.9), kind=kLoop, calls=%fused_computation.11 | loop fusion | flops 8380416 | bytes 21037056 | tf_op jit(solution)/shard_map/reduce_sum | solution.py:82
  515.7 2.3 fusion.10
  (21 shorter events, 0.1 us)
Async XLA Ops:
  8.0 1.4 copy-start
  8.0 467.3 %reduce-scatter.2.cloned.1.call-start = ((), (), s32[]{:S(2)}) async-start(), calls=%async_computation.1 | async-start | bytes 557056 | tf_op jit(solution)/shard_map/reduce_scatter | solution.py:76
  40.3 8.0 %copy-start.2 = (f32[512,8192]{1,0:T(8,128)}, f32[512,8192]{1,0:T(8,128)S(1)}, u32[]{:S(2)}) copy-start(f32[512,8192]{1,0:T(8,128)S(1)} %multiply_exponential_fusion) | copy-start | bytes 50331652
  253.9 35.6 %copy-start.3 = (bf16[256,8192]{1,0:T(8,128)(2,1)S(1)}, bf16[256,8192]{1,0:T(8,128)(2,1)}, u32[]{:S(2)}) copy-start(bf16[256,8192]{1,0:T(8,128)(2,1)} %param.9) | copy-start | bytes 12582916
  289.5 38.4 %copy-start.7 = (u32[128]{0:T(128)S(1)}, u32[128]{0:T(128)}, u32[]{:S(2)}) copy-start(u32[128]{0:T(128)} %constant.44) | copy-start | bytes 1540
  289.5 39.6 %copy-start.6 = (bf16[32]{0:T(256)(128)(2,1)S(1)}, bf16[32]{0:T(256)(128)(2,1)}, u32[]{:S(2)}) copy-start(bf16[32]{0:T(256)(128)(2,1)} %param.11) | copy-start | bytes 196
  358.4 17.7 %copy-start.4 = (bf16[256,8192]{1,0:T(8,128)(2,1)S(1)}, bf16[256,8192]{1,0:T(8,128)(2,1)}, u32[]{:S(2)}) copy-start(bf16[256,8192]{1,0:T(8,128)(2,1)} %param.9) | copy-start | bytes 12582916
  372.9 3.2 copy-start.5
  379.3 130.5 %all-reduce.5.cloned.1.call-start = ((), (), s32[]{:S(2)}) async-start(), calls=%async_computation.2 | async-start | bytes 16777216 | tf_op jit(solution)/shard_map/psum | solution.py:81
  476.2 41.8 %copy-start.1 = (bf16[256,256]{1,0:T(8,128)(2,1)S(1)}, bf16[256,256]{1,0:T(8,128)(2,1)}, u32[]{:S(2)}) copy-start(bf16[256,256]{1,0:T(8,128)(2,1)} %param.7) | copy-start | bytes 393220
Sparse Core Ops, SparseCore 0:
  379.4 87.7 reduce-scatter.1
Sparse Core Ops, SparseCore 1:
  388.5 121.3 all-reduce.4
where the time goes:
time: 536 us; the launch traced here: 527 us
  blocking collectives  331 us (62%)
  matrix products  108 us (20%)
  waiting for transfers between devices  32.1 us (6%)
  other arithmetic  30.5 us (6%)
  between operations  18.9 us (4%)
  local copies, waits for them, and re-layouts  6.24 us (1%)
    psum x3, blocking collectives, on_device(): scale_rows = 1.0 / lax.psum(row_part, 'proto')  90.4 us
    psum x3, blocking collectives, on_device(): scale_cols = 1.0 / lax.psum(col_part, 'patch')  88 us
    psum x1, blocking collectives, on_device(): lax.psum((loss_partial, jnp.sum(row_weight.astype(jnp.float32))), ('patch...  85 us
    dot_general x3, matrix products, on_device(): row_part = jnp.dot(teacher_exp, scale_cols, precision=highest)  53 us
    psum x1, waiting for transfers between devices, on_device(): head_full = lax.psum(head_term(student_rows, grad_logits), 'patch')  32 us
    dot_general x3, matrix products, on_device(): col_part = jnp.dot(scale_rows, teacher_exp, precision=highest)  30.8 us
    unnamed x1, blocking collectives  29 us
    all_gather x1, blocking collectives, on_device(): lax.all_gather(own_teacher, 'proto', axis=0, tiled=True)  20.8 us
  transfers between devices with their start and end apart: 2, of which 1 were waited for; matrix products, arithmetic and copies ran while one was open for 2% of the time, Pallas kernels for 0%

commit v1 on v0

--- a/solution.py
+++ b/solution.py
@@ -7,6 +7,24 @@
 eps = 1e-06
 teacher_temp = 0.07
 student_temp = 0.1
+
+
+def ring_gather(shard, axis, dim):
+    ways, here, turn = (lax.axis_size(axis), lax.axis_index(axis), shard.shape[dim])
+    lengths = [n * ways if d == dim else n for d, n in enumerate(shard.shape)]
+    full = lax.dynamic_update_slice_in_dim(
+        jnp.zeros(lengths, shard.dtype), shard, here * turn, axis=dim
+    )
+    going_up = going_down = shard
+    for far in range(1, ways // 2 + 1):
+        going_up = lax.ppermute(going_up, axis, [(d, (d + 1) % ways) for d in range(ways)])
+        full = lax.dynamic_update_slice_in_dim(full, going_up, (here - far) % ways * turn, axis=dim)
+        if 2 * far < ways:
+            going_down = lax.ppermute(going_down, axis, [(d, (d - 1) % ways) for d in range(ways)])
+            full = lax.dynamic_update_slice_in_dim(
+                full, going_down, (here + far) % ways * turn, axis=dim
+            )
+    return full
 
 
 def unit_rows(values):
@@ -53,7 +71,7 @@
     unit_proto = w_float * col_inverse[None, :]
     proto_unit = unit_proto.astype(jnp.bfloat16)
     teacher_rows, student_rows, weights = (
-        lax.all_gather(own_teacher, "proto", axis=0, tiled=True),
+        ring_gather(own_teacher, "proto", 0),
         lax.all_gather(own_student, "proto", axis=0, tiled=True),
         lax.all_gather(row_weight, "proto", axis=0, tiled=True),
     )

time: 536 us -> 568 us (1.060)
  starting transfers between devices: 0.08 us -> 36.5 us
  blocking collectives: 331 us -> 312 us
  waiting for transfers between devices: 32.1 us -> 45 us
    ppermute x0 -> x15, starting transfers between devices: none -> 36.1 us  [the longest x7 33.7 us: ring_gather(): lax.ppermute(going_down, axis, [(d, (d - 1) % ways) for d in range(ways)])]
    all_gather x1 -> x0, blocking collectives: 20.8 us -> none  [on_device(): lax.all_gather(own_teacher, 'proto', axis=0, tiled=True)]
    psum x3, blocking collectives: 88 us -> 104 us  [on_device(): scale_cols = 1.0 / lax.psum(col_part, 'patch')]
    ppermute x0 -> x15, waiting for transfers between devices: none -> 12.9 us  [the longest x8 12.9 us: ring_gather(): lax.ppermute(going_up, axis, [(d, (d + 1) % ways) for d in range(ways)])]
    psum x1, blocking collectives: 85 us -> 73.1 us  [on_device(): lax.psum((loss_partial, jnp.sum(row_weight.astype(jnp.float32))), ('patch...]
  transfers between devices with their start and end apart: 2 -> 17, of which waited for: 1 -> 8; matrix products, arithmetic and copies ran while one was open for 2% -> 5% of each run, Pallas kernels for 0% -> 0%
where the time goes in v1:
time: 568 us; the launch traced here: 560 us
  blocking collectives  312 us (55%)
  matrix products  110 us (19%)
  waiting for transfers between devices  45 us (8%)
  starting transfers between devices  36.5 us (6%)
  other arithmetic  30.6 us (5%)
  between operations  19.3 us (3%)
  local copies, waits for them, and re-layouts  6.31 us (1%)
    psum x3, blocking collectives, on_device(): scale_cols = 1.0 / lax.psum(col_part, 'patch')  104 us
    psum x3, blocking collectives, on_device(): scale_rows = 1.0 / lax.psum(row_part, 'proto')  87.4 us
    psum x1, blocking collectives, on_device(): lax.psum((loss_partial, jnp.sum(row_weight.astype(jnp.float32))), ('patch...  73.1 us
    dot_general x3, matrix products, on_device(): row_part = jnp.dot(teacher_exp, scale_cols, precision=highest)  52.8 us
    ppermute x7, starting transfers between devices, ring_gather(): lax.ppermute(going_down, axis, [(d, (d - 1) % ways) for d in range(ways)])  33.7 us
    psum x1, waiting for transfers between devices, on_device(): head_full = lax.psum(head_term(student_rows, grad_logits), 'patch')  32 us
    unnamed x1, blocking collectives  30.9 us
    dot_general x3, matrix products, on_device(): col_part = jnp.dot(scale_rows, teacher_exp, precision=highest)  30.8 us
  transfers between devices with their start and end apart: 17, of which 8 were waited for; matrix products, arithmetic and copies ran while one was open for 5% of the time, Pallas kernels for 0%

profile of v1, /device:TPU:1, one launch (start us, length us, event | category | flops | bytes accessed | tf_op | source)
XLA Modules:
  0.0 559.8 jit_solution(8909379708213916753)
XLA Ops:
  8.1 0.7 compare_select_fusion
  8.8 0.7 compare_and_fusion
  9.4 0.6 gather_fusion
  10.1 1.5 gather_fusion.1
  11.9 2.2 collective-permute-start
  14.1 5.0 collective-permute-start.1
  19.1 3.1 fusion
  22.2 16.5 %all_gather.7 = bf16[512,256]{1,0:T(8,128)(2,1)S(1)} all-gather(bf16[32,256]{1,0:T(8,128)(2,1)S(1)} %fusion.13), channel_id=1, replica_groups=mesh['patch'=8,'proto'=16] {'proto'}, dimensions={0}, use_global_device_ids=true | all-gather | bytes 278528 | tf_op jit(solution)/shard_map/all_gather | solution.py:75
  38.7 10.0 %exponential_reduce_fusion = (f32[512]{0:T(512)S(1)}, f32[512,8192]{1,0:T(8,128)}) fusion(bf16[512,256]{1,0:T(8,128)(2,1)S(1)} %all_gather.7, f32[8192]{0:T(1024)S(1)} %add_rsqrt_fusion, bf16[256,8192]{1,0:T(8,128)(2,1)} %param.9), kind=kOutput, calls=%fused_computation.6 | convolution fusion | flops 2162163200 | bytes 21268480 | tf_op jit(solution)/shard_map/dot_general | solution.py:88
  48.8 0.6 dynamic-slice
  50.3 30.9 %all-reduce = bf16[512]{0:T(512)(128)(2,1)S(1)} all-reduce(bf16[512]{0:T(512)(128)(2,1)S(1)} %dynamic-update-slice), channel_id=1, replica_groups=mesh['patch'=8,'proto'=16] {'proto'}, use_global_device_ids=true, to_apply=%add | all-reduce | flops 512 | bytes 2048
  81.4 4.8 collective-permute-start.3
  86.1 1.1 collective-permute-done.2
  87.3 4.8 collective-permute-start.5
  92.1 1.1 collective-permute-done.4
  93.2 4.8 collective-permute-start.7
  98.0 1.1 collective-permute-done.6
  99.1 4.8 collective-permute-start.9
  103.9 1.1 collective-permute-done.8
  105.0 4.8 collective-permute-start.11
  109.8 1.1 collective-permute-done.10
  110.9 4.8 collective-permute-start.13
  115.7 1.1 collective-permute-done.12
  117.1 6.2 %collective-permute-done.14 = bf16[32,256]{1,0:T(8,128)(2,1)S(1)} collective-permute-done((bf16[32,256]{1,0:T(8,128)(2,1)S(1)}, bf16[32,256]{1,0:T(8,128)(2,1)S(1)}, u32[]{:S(2)}, u32[]{:S(2)}) %collective-permute-start.14) | collective-permute-done | bytes 16416 | tf_op jit(solution)/shard_map/ppermute | solution.py:20
  123.3 4.4 multiply_exponential_fusion
  127.8 7.9 %fusion.20 = f32[1,8192]{1,0:T(1,128)S(1)} fusion(f32[512,8192]{1,0:T(8,128)S(1)} %multiply_exponential_fusion), kind=kOutput, calls=%fused_computation.57 | convolution fusion | flops 50331648 | bytes 16809984 | tf_op jit(solution)/shard_map/dot_general | solution.py:84
  135.7 42.2 %psum.71 = f32[8192]{0:T(1024)S(1)} all-reduce(f32[8192]{0:T(1024)S(1)} %bitcast.33), channel_id=1, replica_groups=mesh['patch'=8,'proto'=16] {'patch'}, use_global_device_ids=true, to_apply=%region_5.7 | all-reduce | flops 8192 | bytes 65536 | tf_op jit(solution)/shard_map/psum | solution.py:85
  177.9 17.6 %fusion.24 = f32[1,512]{1,0:T(1,128)S(1)} fusion(f32[512,8192]{1,0:T(8,128)} %copy-done.2, f32[8192,1]{0,1:T(1,128)S(1)} %bitcast.29), kind=kOutput, calls=%fused_computation.66 | convolution fusion | flops 50331648 | bytes 16812032 | tf_op jit(solution)/shard_map/dot_general | solution.py:86
  195.5 28.5 %psum.72 = f32[512]{0:T(512)S(1)} all-reduce(f32[512]{0:T(512)S(1)} %bitcast.35), channel_id=1, replica_groups=mesh['patch'=8,'proto'=16] {'proto'}, use_global_device_ids=true, to_apply=%region_6.8 | all-reduce | flops 512 | bytes 4096 | tf_op jit(solution)/shard_map/psum | solution.py:87
  224.1 11.5 %fusion.25 = f32[1,8192]{1,0:T(1,128)S(1)} fusion(f32[512,1]{0,1:T(1,128)S(1)} %bitcast.37, f32[512,8192]{1,0:T(8,128)} %copy-done.2), kind=kOutput, calls=%fused_computation.67 | convolution fusion | flops 50331648 | bytes 16812032 | tf_op jit(solution)/shard_map/dot_general | solution.py:84
  235.5 30.7 %psum.73 = f32[8192]{0:T(1024)S(1)} all-reduce(f32[8192]{0:T(1024)S(1)} %bitcast.30), channel_id=1, replica_groups=mesh['patch'=8,'proto'=16] {'patch'}, use_global_device_ids=true, to_apply=%region_7.9 | all-reduce | flops 8192 | bytes 65536 | tf_op jit(solution)/shard_map/psum | solution.py:85
  266.2 17.6 %fusion.26 = f32[1,512]{1,0:T(1,128)S(1)} fusion(f32[512,8192]{1,0:T(8,128)} %copy-done.2, f32[8192,1]{0,1:T(1,128)S(1)} %bitcast.31), kind=kOutput, calls=%fused_computation.68 | convolution fusion | flops 50331648 | bytes 16812032 | tf_op jit(solution)/shard_map/dot_general | solution.py:86
  283.9 30.4 %psum.74 = f32[512]{0:T(512)S(1)} all-reduce(f32[512]{0:T(512)S(1)} %bitcast.36), channel_id=1, replica_groups=mesh['patch'=8,'proto'=16] {'proto'}, use_global_device_ids=true, to_apply=%region_8.10 | all-reduce | flops 512 | bytes 4096 | tf_op jit(solution)/shard_map/psum | solution.py:87
  314.2 11.5 %fusion.27 = f32[1,8192]{1,0:T(1,128)S(1)} fusion(f32[512,1]{0,1:T(1,128)S(1)} %bitcast.38, f32[512,8192]{1,0:T(8,128)} %copy-done.2), kind=kOutput, calls=%fused_computation.69 | convolution fusion | flops 50331648 | bytes 16812032 | tf_op jit(solution)/shard_map/dot_general | solution.py:84
  325.7 30.9 %psum.75 = f32[8192]{0:T(1024)S(1)} all-reduce(f32[8192]{0:T(1024)S(1)} %bitcast.32), channel_id=1, replica_groups=mesh['patch'=8,'proto'=16] {'patch'}, use_global_device_ids=true, to_apply=%region_9.11 | all-reduce | flops 8192 | bytes 65536 | tf_op jit(solution)/shard_map/psum | solution.py:85
  356.6 17.6 %fusion.28 = f32[1,512]{1,0:T(1,128)S(1)} fusion(f32[512,8192]{1,0:T(8,128)} %copy-done.2, f32[8192,1]{0,1:T(1,128)S(1)} %bitcast.28), kind=kOutput, calls=%fused_computation.70 | convolution fusion | flops 50331648 | bytes 16812032 | tf_op jit(solution)/shard_map/dot_general | solution.py:86
  374.2 28.5 %all-reduce.2 = (f32[512]{0:T(512)S(1)}, f32[512]{0:T(512)S(1)}) all-reduce(f32[512]{0:T(512)S(1)} %bitcast.34, f32[512]{0:T(512)S(1)} %get-tuple-element.16), channel_id=1, replica_groups=mesh['patch'=8,'proto'=16] {'proto'}, use_global_device_ids=true, to_apply=%region_10.12 | all-reduce | flops 1024 | bytes 8192 | tf_op jit(solution)/shard_map/psum | solution.py:87
  402.7 14.4 %multiply_reduce_fusion = (f32[]{:T(128)}, bf16[512,8192]{1,0:T(8,128)(2,1)S(1)}) fusion(f32[512,8192]{1,0:T(8,128)} %copy-done.2, f32[512,8192]{1,0:T(8,128)} %get-tuple-element.17, f32[512]{0:T(512)S(1)} %log.3, f32[8192]{0:T(1024)S(1)} %broadcast_divide_fusion, f32[512]{0:T(512)S(1)} %broadcast_divide_fusion.5, f32[512]{0:T(512)S(1)} %convert_element_type.28, ...), kind=kLoop, calls=%fused_computation.2 | loop fusion | flops 46137344 | bytes 41984004 | tf_op jit(solution)/shard_map/reduce_sum | solution.py:41
  417.2 3.2 copy-done.4
  420.4 3.2 fusion.7
  423.9 9.0 %convolution_multiply_fusion = f32[256,8192]{1,0:T(8,128)} fusion(bf16[512,256]{1,0:T(8,128)(2,1)S(1)} %all_gather.7, bf16[512,8192]{1,0:T(8,128)(2,1)} %copy-done.4), kind=kOutput, calls=%fused_computation.7 | convolution fusion | flops 2149580800 | bytes 17039360 | tf_op jit(solution)/shard_map/dot_general | solution.py:56
  432.9 0.6 convert_reduce_fusion
  433.5 73.1 %all-reduce.1 = (f32[]{:T(128)}, f32[]{:T(128)}) all-reduce(f32[]{:T(128)} %get-tuple-element.12, f32[]{:T(128)} %convert_reduce_fusion), channel_id=1, replica_groups=mesh['patch'=8,'proto'=16] {'patch','proto'}, use_global_device_ids=true, to_apply=%region_16.18 | all-reduce | flops 2 | bytes 16 | tf_op jit(solution)/shard_map/psum | solution.py:103
  508.0 0.9 fusion.14
  509.0 1.5 fusion.16
  510.5 32.0 %all-reduce.5.cloned.1.call-done = f32[256,8192]{1,0:T(8,128)} async-done(((f32[256,8192]{1,0:T(8,128)}), f32[256,8192]{1,0:T(8,128)}) %all-reduce.5.cloned.1.call-update) | async-done | bytes 8388624 | tf_op jit(solution)/shard_map/psum | solution.py:99
  542.5 6.0 %multiply_reduce_fusion.1 = (f32[8192]{0:T(1024)S(1)}, f32[256,8192]{1,0:T(8,128)S(1)}) fusion(f32[256,8192]{1,0:T(8,128)} %all-reduce.5.cloned.1.call-done, f32[8192]{0:T(1024)S(1)} %add_rsqrt_fusion, bf16[256,8192]{1,0:T(8,128)(2,1)} %param.9), kind=kLoop, calls=%fused_computation.11 | loop fusion | flops 8380416 | bytes 21037056 | tf_op jit(solution)/shard_map/reduce_sum | solution.py:100
  548.4 2.3 fusion.10
  (66 shorter events, 1.5 us)
Async XLA Ops:
  8.0 1.4 copy-start
  8.0 500.0 %reduce-scatter.2.cloned.1.call-start = ((), (), s32[]{:S(2)}) async-start(), calls=%async_computation.1 | async-start | bytes 557056 | tf_op jit(solution)/shard_map/reduce_scatter | solution.py:94
  11.9 69.4 %collective-permute-start = (bf16[32,256]{1,0:T(8,128)(2,1)S(1)}, bf16[32,256]{1,0:T(8,128)(2,1)S(1)}, u32[]{:S(2)}, u32[]{:S(2)}) collective-permute-start(bf16[32,256]{1,0:T(8,128)(2,1)S(1)} %get-tuple-element.11), channel_id=1, source_target_pairs={{0,1},{1,2},{2,3},{3,4},{4,5},{5,6},{6,7},{7,8},{8,9},{9,10},{10,1... | collective-permute-start | bytes 49160 | tf_op jit(solution)/shard_map/ppermute | solution.py:20
  14.1 67.3 %collective-permute-start.1 = (bf16[32,256]{1,0:T(8,128)(2,1)S(1)}, bf16[32,256]{1,0:T(8,128)(2,1)S(1)}, u32[]{:S(2)}, u32[]{:S(2)}) collective-permute-start(bf16[32,256]{1,0:T(8,128)(2,1)S(1)} %get-tuple-element.11), channel_id=1, source_target_pairs={{0,15},{1,0},{2,1},{3,2},{4,3},{5,4},{6,5},{7,6},{8,7},{9,8},{10,9... | collective-permute-start | bytes 49160 | tf_op jit(solution)/shard_map/ppermute | solution.py:23
  38.7 10.1 %copy-start.6 = (u32[128]{0:T(128)S(1)}, u32[128]{0:T(128)}, u32[]{:S(2)}) copy-start(u32[128]{0:T(128)} %constant.150) | copy-start | bytes 1540
  38.7 11.3 %copy-start.5 = (bf16[32]{0:T(256)(128)(2,1)S(1)}, bf16[32]{0:T(256)(128)(2,1)}, u32[]{:S(2)}) copy-start(bf16[32]{0:T(256)(128)(2,1)} %param.11) | copy-start | bytes 196
  81.3 6.0 %collective-permute-start.2 = (bf16[32,256]{1,0:T(8,128)(2,1)S(1)}, bf16[32,256]{1,0:T(8,128)(2,1)S(1)}, u32[]{:S(2)}, u32[]{:S(2)}) collective-permute-start(bf16[32,256]{1,0:T(8,128)(2,1)S(1)} %collective-permute-done), channel_id=1, source_target_pairs={{0,1},{1,2},{2,3},{3,4},{4,5},{5,6},{6,7},{7,8},{8,9},{9,10},{10,1... | collective-permute-start | bytes 49160 | tf_op jit(solution)/shard_map/ppermute | solution.py:20
  81.4 5.9 %collective-permute-start.3 = (bf16[32,256]{1,0:T(8,128)(2,1)S(1)}, bf16[32,256]{1,0:T(8,128)(2,1)S(1)}, u32[]{:S(2)}, u32[]{:S(2)}) collective-permute-start(bf16[32,256]{1,0:T(8,128)(2,1)S(1)} %collective-permute-done.1), channel_id=1, source_target_pairs={{0,15},{1,0},{2,1},{3,2},{4,3},{5,4},{6,5},{7,6},{8,7},{9,8},{10,9... | collective-permute-start | bytes 49160 | tf_op jit(solution)/shard_map/ppermute | solution.py:23
  87.3 5.9 %collective-permute-start.4 = (bf16[32,256]{1,0:T(8,128)(2,1)S(1)}, bf16[32,256]{1,0:T(8,128)(2,1)S(1)}, u32[]{:S(2)}, u32[]{:S(2)}) collective-permute-start(bf16[32,256]{1,0:T(8,128)(2,1)S(1)} %collective-permute-done.2), channel_id=1, source_target_pairs={{0,1},{1,2},{2,3},{3,4},{4,5},{5,6},{6,7},{7,8},{8,9},{9,10},{10,1... | collective-permute-start | bytes 49160 | tf_op jit(solution)/shard_map/ppermute | solution.py:20
  87.3 5.9 %collective-permute-start.5 = (bf16[32,256]{1,0:T(8,128)(2,1)S(1)}, bf16[32,256]{1,0:T(8,128)(2,1)S(1)}, u32[]{:S(2)}, u32[]{:S(2)}) collective-permute-start(bf16[32,256]{1,0:T(8,128)(2,1)S(1)} %collective-permute-done.3), channel_id=1, source_target_pairs={{0,15},{1,0},{2,1},{3,2},{4,3},{5,4},{6,5},{7,6},{8,7},{9,8},{10,9... | collective-permute-start | bytes 49160 | tf_op jit(solution)/shard_map/ppermute | solution.py:23
  93.2 5.9 %collective-permute-start.6 = (bf16[32,256]{1,0:T(8,128)(2,1)S(1)}, bf16[32,256]{1,0:T(8,128)(2,1)S(1)}, u32[]{:S(2)}, u32[]{:S(2)}) collective-permute-start(bf16[32,256]{1,0:T(8,128)(2,1)S(1)} %collective-permute-done.4), channel_id=1, source_target_pairs={{0,1},{1,2},{2,3},{3,4},{4,5},{5,6},{6,7},{7,8},{8,9},{9,10},{10,1... | collective-permute-start | bytes 49160 | tf_op jit(solution)/shard_map/ppermute | solution.py:20
  93.2 5.9 %collective-permute-start.7 = (bf16[32,256]{1,0:T(8,128)(2,1)S(1)}, bf16[32,256]{1,0:T(8,128)(2,1)S(1)}, u32[]{:S(2)}, u32[]{:S(2)}) collective-permute-start(bf16[32,256]{1,0:T(8,128)(2,1)S(1)} %collective-permute-done.5), channel_id=1, source_target_pairs={{0,15},{1,0},{2,1},{3,2},{4,3},{5,4},{6,5},{7,6},{8,7},{9,8},{10,9... | collective-permute-start | bytes 49160 | tf_op jit(solution)/shard_map/ppermute | solution.py:23
  99.1 5.9 %collective-permute-start.8 = (bf16[32,256]{1,0:T(8,128)(2,1)S(1)}, bf16[32,256]{1,0:T(8,128)(2,1)S(1)}, u32[]{:S(2)}, u32[]{:S(2)}) collective-permute-start(bf16[32,256]{1,0:T(8,128)(2,1)S(1)} %collective-permute-done.6), channel_id=1, source_target_pairs={{0,1},{1,2},{2,3},{3,4},{4,5},{5,6},{6,7},{7,8},{8,9},{9,10},{10,1... | collective-permute-start | bytes 49160 | tf_op jit(solution)/shard_map/ppermute | solution.py:20
  99.1 5.9 %collective-permute-start.9 = (bf16[32,256]{1,0:T(8,128)(2,1)S(1)}, bf16[32,256]{1,0:T(8,128)(2,1)S(1)}, u32[]{:S(2)}, u32[]{:S(2)}) collective-permute-start(bf16[32,256]{1,0:T(8,128)(2,1)S(1)} %collective-permute-done.7), channel_id=1, source_target_pairs={{0,15},{1,0},{2,1},{3,2},{4,3},{5,4},{6,5},{7,6},{8,7},{9,8},{10,9... | collective-permute-start | bytes 49160 | tf_op jit(solution)/shard_map/ppermute | solution.py:23
  105.0 5.9 %collective-permute-start.10 = (bf16[32,256]{1,0:T(8,128)(2,1)S(1)}, bf16[32,256]{1,0:T(8,128)(2,1)S(1)}, u32[]{:S(2)}, u32[]{:S(2)}) collective-permute-start(bf16[32,256]{1,0:T(8,128)(2,1)S(1)} %collective-permute-done.8), channel_id=1, source_target_pairs={{0,1},{1,2},{2,3},{3,4},{4,5},{5,6},{6,7},{7,8},{8,9},{9,10},{10,1... | collective-permute-start | bytes 49160 | tf_op jit(solution)/shard_map/ppermute | solution.py:20
  105.0 5.9 %collective-permute-start.11 = (bf16[32,256]{1,0:T(8,128)(2,1)S(1)}, bf16[32,256]{1,0:T(8,128)(2,1)S(1)}, u32[]{:S(2)}, u32[]{:S(2)}) collective-permute-start(bf16[32,256]{1,0:T(8,128)(2,1)S(1)} %collective-permute-done.9), channel_id=1, source_target_pairs={{0,15},{1,0},{2,1},{3,2},{4,3},{5,4},{6,5},{7,6},{8,7},{9,8},{10,9... | collective-permute-start | bytes 49160 | tf_op jit(solution)/shard_map/ppermute | solution.py:23
  110.9 5.9 %collective-permute-start.12 = (bf16[32,256]{1,0:T(8,128)(2,1)S(1)}, bf16[32,256]{1,0:T(8,128)(2,1)S(1)}, u32[]{:S(2)}, u32[]{:S(2)}) collective-permute-start(bf16[32,256]{1,0:T(8,128)(2,1)S(1)} %collective-permute-done.10), channel_id=1, source_target_pairs={{0,1},{1,2},{2,3},{3,4},{4,5},{5,6},{6,7},{7,8},{8,9},{9,10},{10,1... | collective-permute-start | bytes 49160 | tf_op jit(solution)/shard_map/ppermute | solution.py:20
  110.9 6.1 %collective-permute-start.13 = (bf16[32,256]{1,0:T(8,128)(2,1)S(1)}, bf16[32,256]{1,0:T(8,128)(2,1)S(1)}, u32[]{:S(2)}, u32[]{:S(2)}) collective-permute-start(bf16[32,256]{1,0:T(8,128)(2,1)S(1)} %collective-permute-done.11), channel_id=1, source_target_pairs={{0,15},{1,0},{2,1},{3,2},{4,3},{5,4},{6,5},{7,6},{8,7},{9,8},{10,9... | collective-permute-start | bytes 49160 | tf_op jit(solution)/shard_map/ppermute | solution.py:23
  116.8 6.5 %collective-permute-start.14 = (bf16[32,256]{1,0:T(8,128)(2,1)S(1)}, bf16[32,256]{1,0:T(8,128)(2,1)S(1)}, u32[]{:S(2)}, u32[]{:S(2)}) collective-permute-start(bf16[32,256]{1,0:T(8,128)(2,1)S(1)} %collective-permute-done.12), channel_id=1, source_target_pairs={{0,1},{1,2},{2,3},{3,4},{4,5},{5,6},{6,7},{7,8},{8,9},{9,10},{10,1... | collective-permute-start | bytes 49160 | tf_op jit(solution)/shard_map/ppermute | solution.py:20
  127.7 8.0 %copy-start.2 = (f32[512,8192]{1,0:T(8,128)}, f32[512,8192]{1,0:T(8,128)S(1)}, u32[]{:S(2)}) copy-start(f32[512,8192]{1,0:T(8,128)S(1)} %multiply_exponential_fusion) | copy-start | bytes 50331652
  402.7 17.7 %copy-start.3 = (bf16[256,8192]{1,0:T(8,128)(2,1)S(1)}, bf16[256,8192]{1,0:T(8,128)(2,1)}, u32[]{:S(2)}) copy-start(bf16[256,8192]{1,0:T(8,128)(2,1)} %param.9) | copy-start | bytes 12582916
  417.2 3.2 copy-start.4
  423.6 118.9 %all-reduce.5.cloned.1.call-start = ((), (), s32[]{:S(2)}) async-start(), calls=%async_computation.2 | async-start | bytes 16777216 | tf_op jit(solution)/shard_map/psum | solution.py:99
  508.9 41.8 %copy-start.1 = (bf16[256,256]{1,0:T(8,128)(2,1)S(1)}, bf16[256,256]{1,0:T(8,128)(2,1)}, u32[]{:S(2)}) copy-start(bf16[256,256]{1,0:T(8,128)(2,1)} %param.7) | copy-start | bytes 393220
Sparse Core Ops, SparseCore 0:
  423.7 75.9 reduce-scatter.1
Sparse Core Ops, SparseCore 1:
  433.0 109.4 all-reduce.4
